TPU v7x, 32 devices: a whole 2x2x4 slice. The times are simulated.
32 devices in a mesh: rep: 2 (over x), tbl: 16 (over z, y, core).
Axes of the slice: x: 2, y: 2, z: 4, core: 2. Of those that a mesh axis runs over, the one named last changes fastest.
Arguments:
- embeddings: bfloat16 [131072, 256], P('tbl'), may hold values from -6 to 6
- raw_ids: int32 [128, 16, 60], P('tbl', 'rep'), may hold values from 0 to 16383
- id_weights: bfloat16 [128, 16, 60], P('tbl', 'rep'), may hold values from 0.25 to 4
- lengths: int32 [128, 16], P('tbl', 'rep'), may hold values from 1 to 60
- table_slot: int32 [16], replicated, may hold values from 0 to 15, each once
- table_rows: int32 [16], replicated, may hold values from 1 to 8192, 32768 in all
Outputs:
- pooled: float32 [128, 16, 256], P('tbl', 'rep')
Inputs may be any that keep to these rules, and one draw needn't show every extreme that they name: The bag of request q for table k holds its first lengths[q, k] ids. `table_slot`: each slot holds exactly one table. `table_rows`: some table uses all 8192 rows of its slot.
All inputs are finite; a program needn't handle non-finite values.
Results may differ from a plain program's by a relative error of at most 0.0003.
Values sent between devices are 32-bit elements; how exact they have to be, the bound alone decides.
No kernel may reach another device: no remote copies, remote signals or barrier semaphores. Data moves between devices by JAX's collectives and lax.ppermute only.
A program may use at most 64 MiB of HBM per device.

v0:
```python
import math

import jax
import jax.numpy as jnp
from jax import lax
from jax.sharding import PartitionSpec as P

TBL_DEV = 1
ROWS_SLOT = 8192


def pool_block(embeddings, row_block, weight_block, len_block):
    picked = jnp.take(embeddings, row_block, axis=0)
    live = (
        lax.broadcasted_iota(jnp.int32, row_block.shape, row_block.ndim - 1) < len_block[..., None]
    )
    scaled = jnp.where(live, weight_block, jnp.zeros_like(weight_block))
    summed = jnp.einsum(
        "giqb,giqbd->giqd", scaled, picked.astype(jnp.float32), preferred_element_type=jnp.float32
    )
    divisor = jnp.maximum(len_block, 1).astype(jnp.float32)[..., None]
    return summed / divisor


def pool_rows(embeddings, targets, weighting, counts):
    sources, members, queries, positions = targets.shape
    blocking = math.gcd(sources, 16)
    shaped = targets.reshape(sources // blocking, blocking, members, queries, positions)
    weighted = weighting.reshape(sources // blocking, blocking, members, queries, positions)
    counted = counts.reshape(sources // blocking, blocking, members, queries)

    def pool_group(operands):
        return pool_block(embeddings, operands[0], operands[1], operands[2])

    pooled = lax.map(pool_group, (shaped, weighted, counted))
    return pooled.reshape(sources, members, queries, embeddings.shape[1])


def per_device(embeddings, raw_ids, id_weights, lengths, table_slot, table_rows):
    replicas = lax.axis_size("rep")
    replica = lax.axis_index("rep")
    tables = table_slot.shape[0]
    tables_each = tables // replicas
    shards = tables // TBL_DEV
    order = jnp.arange(tables, dtype=jnp.int32)
    slot_table = jnp.zeros((tables,), jnp.int32).at[table_slot].set(order)
    offsets = order % TBL_DEV * ROWS_SLOT
    sizes_by_slot = table_rows[slot_table]
    first = replica * tables_each
    within = jnp.clip(slot_table - first, 0, tables_each - 1)
    owned = (slot_table >= first) & (slot_table < first + tables_each)
    picked_ids = jnp.take(raw_ids, within, axis=1)
    picked_weights = jnp.take(id_weights, within, axis=1).astype(jnp.float32)
    picked_counts = jnp.where(owned[None, :], jnp.take(lengths, within, axis=1), 0)
    queries = picked_ids.shape[0]
    width = picked_ids.shape[2]
    targets = offsets[None, :, None] + picked_ids % sizes_by_slot[None, :, None]
    targets = (
        jnp.transpose(targets, (1, 0, 2))
        .reshape(shards, TBL_DEV, queries, width)
        .astype(jnp.float32)
    )
    weights_sent = jnp.transpose(picked_weights, (1, 0, 2)).reshape(shards, TBL_DEV, queries, width)
    counts_sent = jnp.transpose(picked_counts).reshape(shards, TBL_DEV, queries).astype(jnp.float32)
    row_index = lax.all_to_all(targets, "tbl", split_axis=0, concat_axis=0, tiled=True).astype(
        jnp.int32
    )
    live_count = lax.all_to_all(counts_sent, "tbl", split_axis=0, concat_axis=0, tiled=True).astype(
        jnp.int32
    )
    pooled = pool_rows(
        embeddings,
        row_index,
        lax.all_to_all(weights_sent, "tbl", split_axis=0, concat_axis=0, tiled=True),
        live_count,
    )
    by_slot = lax.all_to_all(pooled, "tbl", split_axis=0, concat_axis=0, tiled=True)
    by_slot = by_slot.reshape(tables, queries, embeddings.shape[1])
    mine = lax.dynamic_slice_in_dim(table_slot, first, tables_each)
    return jnp.transpose(jnp.take(by_slot, mine, axis=0), (1, 0, 2))


def solution(mesh):
    in_specs = (
        P("tbl", None),
        P("tbl", "rep", None),
        P("tbl", "rep", None),
        P("tbl", "rep"),
        P(),
        P(),
    )
    out_specs = P("tbl", "rep", None)
    return jax.shard_map(
        per_device, mesh=mesh, in_specs=in_specs, out_specs=out_specs, check_vma=False
    )
```

profile of v0, /device:TPU:0, one launch (start us, length us, event | category | flops | bytes accessed | tf_op | source)
XLA Modules:
  0.0 84.4 jit_solution(1635872264291782984)
XLA Ops:
  0.0 0.0 copy-start
  0.0 0.7 compare_select_fusion.4
  0.7 0.6 scatter_custom_fusion
  1.3 1.3 %gather_fusion.3 = s32[16]{0:T(128)S(1)} fusion(s32[16]{0:T(128)} %param.11, s32[1024]{0:T(1024)S(1)} %pad_clamp_fusion.2), kind=kCustom, calls=%fused_computation.3 | custom fusion | bytes 192 | tf_op jit(solution)/shard_map/gather | solution.py:48
  2.7 0.8 copy.26
  3.4 0.6 gather_fusion
  4.0 0.1 copy.27
  4.1 0.7 copy.28
  4.8 7.4 %all-to-all-start = ((f32[16,1,8]{2,1,0:T(1,128)}), f32[16,1,8]{2,1,0:T(1,128)S(1)}, u32[]{:S(2)}, u32[]{:S(2)}) async-start(f32[16,1,8]{2,1,0:T(1,128)} %copy.28), calls=%async_computation | async-start | bytes 16384 | tf_op jit(solution)/shard_map/all_to_all | solution.py:68
  12.2 1.4 %gather_fusion.1 = bf16[16,8,60]{2,0,1:T(8,128)(2,1)S(1)} fusion(bf16[8,8,60]{2,1,0:T(8,128)(2,1)} %param.8, s32[1024]{0:T(1024)S(1)} %pad_clamp_fusion.3), kind=kCustom, calls=%fused_computation.1 | custom fusion | bytes 30784 | tf_op jit(solution)/shard_map/jit(_take)/gather | solution.py:53
  13.6 0.0 copy-done
  13.6 0.6 gather_fusion.2
  14.2 0.7 fusion.6
  15.0 0.1 bitcast_convert_fusion
  15.1 0.8 reshape.158
  15.9 0.8 reshape.160
  16.6 2.0 %all-to-all-done = f32[16,1,8]{2,1,0:T(1,128)S(1)} async-done(((f32[16,1,8]{2,1,0:T(1,128)}), f32[16,1,8]{2,1,0:T(1,128)S(1)}, u32[]{:S(2)}, u32[]{:S(2)}) %all-to-all-start) | async-done | bytes 544 | tf_op jit(solution)/shard_map/all_to_all | solution.py:68
  18.6 4.0 %all-to-all-start.2 = ((f32[16,1,480]{2,1,0:T(1,128)}), f32[16,1,480]{2,1,0:T(1,128)S(1)}, u32[]{:S(2)}, u32[]{:S(2)}) async-start(f32[16,1,480]{2,1,0:T(1,128)} %reshape.160), calls=%async_computation.2 | async-start | bytes 65536 | tf_op jit(solution)/shard_map/all_to_all | solution.py:65
  22.6 0.1 copy.29
  22.7 0.1 copy.30
  22.8 0.1 copy.33
  22.9 6.4 %all-to-all-done.2 = f32[16,1,480]{2,1,0:T(1,128)S(1)} async-done(((f32[16,1,480]{2,1,0:T(1,128)}), f32[16,1,480]{2,1,0:T(1,128)S(1)}, u32[]{:S(2)}, u32[]{:S(2)}) %all-to-all-start.2) | async-done | bytes 30752 | tf_op jit(solution)/shard_map/all_to_all | solution.py:65
  29.3 3.5 %all-to-all-start.1 = ((f32[16,1,480]{2,1,0:T(1,128)}), f32[16,1,480]{2,1,0:T(1,128)S(1)}, u32[]{:S(2)}, u32[]{:S(2)}) async-start(f32[16,1,480]{2,1,0:T(1,128)} %reshape.158), calls=%async_computation.1 | async-start | bytes 65536 | tf_op jit(solution)/shard_map/all_to_all | solution.py:74
  32.8 0.5 broadcast.215
  33.3 0.7 reduce.1
  34.0 0.1 reshape.161
  34.2 5.2 %all-to-all-done.1 = f32[16,1,480]{2,1,0:T(1,128)S(1)} async-done(((f32[16,1,480]{2,1,0:T(1,128)}), f32[16,1,480]{2,1,0:T(1,128)S(1)}, u32[]{:S(2)}, u32[]{:S(2)}) %all-to-all-start.1) | async-done | bytes 30752 | tf_op jit(solution)/shard_map/all_to_all | solution.py:74
  39.4 0.7 reduce
  40.1 0.1 reshape.159
  40.2 0.1 reshape.121
  40.3 21.0 %gather_fusion.4 = bf16[7680,256]{1,0:T(8,128)(2,1)} fusion(bf16[8192,256]{1,0:T(8,128)(2,1)} %param.6, s32[8192]{0:T(1024)S(1)} %pad_clamp_fusion), kind=kCustom, calls=%fused_computation.4 | custom fusion | bytes 7895040 | tf_op jit(solution)/shard_map/while/body/eval_jaxpr/jit(_take)/gather | solution.py:13
  61.3 6.5 %gather.31 = bf16[16,8,60,256]{3,2,1,0:T(8,128)(2,1)} reshape(bf16[7680,256]{1,0:T(8,128)(2,1)} %gather_fusion.4) | data formatting | bytes 7864320 | tf_op jit(solution)/shard_map/while/body/eval_jaxpr/jit(_take)/gather | solution.py:13
  67.8 0.0 copy-start.1
  67.8 0.1 fusion.7
  67.9 3.1 %fusion = f32[16,8,1,256]{3,2,1,0:T(1,128)S(1)} fusion(f32[16,8,60,1]{2,3,1,0:T(1,128)S(1)} %bitcast.31, bf16[16,8,60,256]{3,2,1,0:T(8,128)(2,1)} %gather.31, pred[16,8,60]{2,1,0:T(8,128)(4,1)S(1)} %and_bitcast_fusion), kind=kOutput, calls=%fused_computation.7 | convolution fusion | flops 5898240 | bytes 4101632 | tf_op jit(solution)/shard_map/while/body/eval_jaxpr/giqb,giqbd->giqd/dot_general | solution.py:18
  71.0 0.7 fusion.4
  71.7 3.5 %all-to-all-start.3 = ((f32[16,1,8,256]{3,2,1,0:T(8,128)}), f32[16,1,8,256]{3,2,1,0:T(8,128)S(1)}, u32[]{:S(2)}, u32[]{:S(2)}) async-start(f32[16,1,8,256]{3,2,1,0:T(8,128)} %fusion.4), calls=%async_computation.3 | async-start | bytes 262144 | tf_op jit(solution)/shard_map/all_to_all | solution.py:77
  75.2 0.0 copy-done.1
  75.3 0.1 compare_and_fusion.2
  75.3 7.8 %all-to-all-done.3 = f32[16,1,8,256]{3,2,1,0:T(8,128)S(1)} async-done(((f32[16,1,8,256]{3,2,1,0:T(8,128)}), f32[16,1,8,256]{3,2,1,0:T(8,128)S(1)}, u32[]{:S(2)}, u32[]{:S(2)}) %all-to-all-start.3) | async-done | bytes 131104 | tf_op jit(solution)/shard_map/all_to_all | solution.py:77
  83.1 0.6 gather_fusion.5
  83.7 0.1 select_bitcast_fusion
  83.8 0.7 copy.34
  (15 shorter events, 0.2 us)
Async XLA Ops:
  0.0 13.6 %copy-start = (s32[8,8,60]{2,1,0:T(8,128)S(1)}, s32[8,8,60]{2,1,0:T(8,128)}, u32[]{:S(2)}) copy-start(s32[8,8,60]{2,1,0:T(8,128)} %param.7) | copy-start | bytes 46084
  4.8 13.9 %all-to-all-start = ((f32[16,1,8]{2,1,0:T(1,128)}), f32[16,1,8]{2,1,0:T(1,128)S(1)}, u32[]{:S(2)}, u32[]{:S(2)}) async-start(f32[16,1,8]{2,1,0:T(1,128)} %copy.28), calls=%async_computation | async-start | bytes 16384 | tf_op jit(solution)/shard_map/all_to_all | solution.py:68
  18.6 10.7 %all-to-all-start.2 = ((f32[16,1,480]{2,1,0:T(1,128)}), f32[16,1,480]{2,1,0:T(1,128)S(1)}, u32[]{:S(2)}, u32[]{:S(2)}) async-start(f32[16,1,480]{2,1,0:T(1,128)} %reshape.160), calls=%async_computation.2 | async-start | bytes 65536 | tf_op jit(solution)/shard_map/all_to_all | solution.py:65
  29.3 10.1 %all-to-all-start.1 = ((f32[16,1,480]{2,1,0:T(1,128)}), f32[16,1,480]{2,1,0:T(1,128)S(1)}, u32[]{:S(2)}, u32[]{:S(2)}) async-start(f32[16,1,480]{2,1,0:T(1,128)} %reshape.158), calls=%async_computation.1 | async-start | bytes 65536 | tf_op jit(solution)/shard_map/all_to_all | solution.py:74
  67.8 7.4 %copy-start.1 = (s32[16]{0:T(128)S(1)}, s32[16]{0:T(128)}, u32[]{:S(2)}) copy-start(s32[16]{0:T(128)} %param.10) | copy-start | bytes 196
  71.7 11.4 %all-to-all-start.3 = ((f32[16,1,8,256]{3,2,1,0:T(8,128)}), f32[16,1,8,256]{3,2,1,0:T(8,128)S(1)}, u32[]{:S(2)}, u32[]{:S(2)}) async-start(f32[16,1,8,256]{3,2,1,0:T(8,128)} %fusion.4), calls=%async_computation.3 | async-start | bytes 262144 | tf_op jit(solution)/shard_map/all_to_all | solution.py:77
where the time goes:
time: 85.1 us; the launch traced here: 84.4 us
  local copies, waits for them, and re-layouts  37.3 us (44%)
  waiting for transfers between devices  21.4 us (25%)
  starting transfers between devices  18.4 us (22%)
  other arithmetic  3.98 us (5%)
  matrix products  3.05 us (4%)
    gather x2, local copies, waits for them, and re-layouts, pool_block(): picked = jnp.take(embeddings, row_block, axis=0)  27.5 us
    all_to_all x1, waiting for transfers between devices, per_device(): lax.all_to_all(pooled, 'tbl', split_axis=0, concat_axis=0, tiled=True)  7.77 us
    all_to_all x1, starting transfers between devices, per_device(): lax.all_to_all(counts_sent, 'tbl', split_axis=0, concat_axis=0, tiled=True)  7.41 us
    all_to_all x1, waiting for transfers between devices, per_device(): lax.all_to_all(targets, 'tbl', split_axis=0, concat_axis=0, tiled=True)  6.4 us
    all_to_all x1, waiting for transfers between devices, per_device(): lax.all_to_all(weights_sent, 'tbl', split_axis=0, concat_axis=0, tiled=True)  5.23 us
    all_to_all x1, starting transfers between devices, per_device(): lax.all_to_all(targets, 'tbl', split_axis=0, concat_axis=0, tiled=True)  4.03 us
    all_to_all x1, starting transfers between devices, per_device(): lax.all_to_all(pooled, 'tbl', split_axis=0, concat_axis=0, tiled=True)  3.51 us
    all_to_all x1, starting transfers between devices, per_device(): lax.all_to_all(weights_sent, 'tbl', split_axis=0, concat_axis=0, tiled=True)  3.5 us
  transfers between devices with their start and end apart: 4, of which 4 were waited for; matrix products, arithmetic and copies ran while one was open for 7% of the time, Pallas kernels for 0%

commit v1 on v0

v1 whole, which is shorter than its diff:
```python
import functools

import jax
import jax.numpy as jnp
from jax import lax
from jax.experimental import pallas as pl
from jax.experimental.pallas import tpu as pltpu
from jax.sharding import PartitionSpec as P

LANES = 128
HALF = 64
SUB = 8
LOW = 256
BLOCK_BAGS = 64


def pack_kernel(slot_ref, rows_ref, ids_ref, weights_ref, len_ref, out_ref, wide_ref):
    queries, members, width = ids_ref.shape
    first = lax.axis_index("rep") * members
    wide_ref[:, 0:width] = weights_ref[...].reshape(queries * members, width).astype(jnp.float32)
    flat_ids = ids_ref.reshape(queries * members, width)
    position = lax.broadcasted_iota(jnp.int32, (queries, width), 1)
    counts = len_ref[...]
    out_ref[...] = jnp.zeros_like(out_ref)
    for member in range(members):
        slot = slot_ref[first + member]
        rows = jnp.full((queries, width), rows_ref[first + member], jnp.int32).astype(jnp.float32)
        ids = flat_ids[pl.ds(member, queries, stride=members), :].astype(jnp.float32)
        local = ids - jnp.floor((ids + 0.5) * (1.0 / rows)) * rows
        count = counts[:, member : member + 1]
        weights = wide_ref[pl.ds(member, queries, stride=members), 0:width]
        weights = jnp.where(position < count, weights, 0.0)
        out_ref[slot, :, 0:width] = local
        out_ref[slot, :, width : width + 1] = count.astype(jnp.float32)
        out_ref[slot, :, HALF : HALF + width] = weights


def pool_kernel(width, slot_ref, msg_ref, emb_ref, out_ref, lhs_ref, rhs_ref, w_ref):
    sources = msg_ref.shape[0]
    tables = slot_ref.shape[0]
    replicas = lax.axis_size("rep")
    here = lax.axis_index("tbl")

    def find(k, owner):
        return jnp.where(slot_ref[k] == here, k // (tables // replicas), owner)

    owner = lax.fori_loop(0, tables, find, jnp.int32(0))
    rows, dim = emb_ref.shape
    highs = rows // LOW
    per = SUB // replicas
    block = min(BLOCK_BAGS, sources * per)
    groups = block // SUB
    lane = lax.broadcasted_iota(jnp.int32, (SUB, LANES), 1)
    sub = lax.broadcasted_iota(jnp.int32, (SUB, LANES), 0)
    left = lane < HALF
    low_iota = lax.broadcasted_iota(jnp.int32, (LOW, LANES), 0).astype(jnp.float32).astype(jnp.bfloat16)

    def gather_group(start):
        one, two = msg_ref[start], msg_ref[start + 1]
        low_half = jnp.where(sub < per, one, pltpu.roll(two, per, 0))
        high_half = jnp.where(sub < per, pltpu.roll(one, per, 0), two)
        return jnp.where(owner == 0, low_half, high_half)

    def one_block(index, carry):
        base = index * (block // per)

        def one_group(g, carry):
            msg = gather_group(base + 2 * g)
            turned = pltpu.roll(msg, HALF, 1)
            ids = jnp.where(left, msg, turned)
            weights = jnp.where(left, turned, msg)
            high = jnp.floor(ids * (1.0 / LOW))
            low = ids - high * LOW
            for m in range(SUB // 2):
                cols = slice(m * LANES, (m + 1) * LANES)
                own = sub == jnp.where(left, 2 * m, 2 * m + 1)
                h = jnp.where(own, high, -100.0)
                h = jnp.concatenate([h, h - 1.0], 0).astype(jnp.bfloat16)
                w = jnp.where(own, weights, 0.0)
                w = jnp.concatenate([w, w], 0).astype(jnp.bfloat16)
                for top in range(0, highs, 2):
                    lhs_ref[top * SUB : (top + 2) * SUB, cols] = jnp.where(
                        h == jnp.bfloat16(top), w, jnp.bfloat16(0)
                    )
                row = jnp.where(left[0:1], low[2 * m : 2 * m + 1], low[2 * m + 1 : 2 * m + 2])
                row = jnp.broadcast_to(row, (16, LANES)).astype(jnp.bfloat16)
                row = jnp.concatenate([row] * (LOW // 16), 0)
                rhs_ref[:, cols] = jnp.where(low_iota == row, jnp.bfloat16(1), jnp.bfloat16(0))
            spread = lax.dot_general(
                lhs_ref[...], rhs_ref[...], (((1,), (1,)), ((), ())), preferred_element_type=jnp.float32
            )
            rest = spread - spread.astype(jnp.bfloat16).astype(jnp.float32)
            at = pl.ds(pl.multiple_of(g * 2 * SUB, 2 * SUB), 2 * SUB)
            for top in range(highs):
                part = slice(top * SUB, (top + 1) * SUB)
                both = jnp.concatenate([spread[part], rest[part]], 0)
                w_ref[at, top * LOW : (top + 1) * LOW] = both.astype(jnp.bfloat16)
            return carry

        lax.fori_loop(0, groups, one_group, 0)
        total = jnp.dot(w_ref[...], emb_ref[...], preferred_element_type=jnp.float32)
        for g in range(groups):
            msg = gather_group(base + 2 * g)
            at = 2 * SUB * g
            pooled = total[at : at + SUB] + total[at + SUB : at + 2 * SUB]
            pooled = pooled / msg[:, width : width + 1]
            first, last = pooled[:, :LANES], pooled[:, LANES:]
            one = jnp.where(sub < per, first, pltpu.roll(last, per, 0))
            two = jnp.where(sub < per, pltpu.roll(first, per, 0), last)
            for replica in range(replicas):
                out_ref[(base + 2 * g) * replicas + replica] = one
                out_ref[(base + 2 * g + 1) * replicas + replica] = two
        return carry

    blocks = sources * per // block
    if blocks == 1:
        one_block(0, 0)
    else:
        lax.fori_loop(0, blocks, one_block, 0)


def place_kernel(slot_ref, by_slot_ref, out_ref):
    queries, members, dim = out_ref.shape
    first = lax.axis_index("rep") * members
    per = by_slot_ref.shape[1] // 2
    upper = lax.broadcasted_iota(jnp.int32, by_slot_ref.shape[1:], 0) < per
    for member in range(members):
        slot = slot_ref[first + member]
        one, two = by_slot_ref[2 * slot], by_slot_ref[2 * slot + 1]
        out_ref[:, member, :LANES] = jnp.where(upper, one, pltpu.roll(two, per, 0))
        out_ref[:, member, LANES:] = jnp.where(upper, pltpu.roll(one, per, 0), two)


def exchange(array):
    return lax.all_to_all(array, ("tbl", "rep"), split_axis=0, concat_axis=0, tiled=True)


def per_device(embeddings, raw_ids, id_weights, lengths, table_slot, table_rows):
    queries, members, width = raw_ids.shape
    tables = table_slot.shape[0]
    rows, dim = embeddings.shape
    vmem = pl.BlockSpec(memory_space=pltpu.VMEM)
    smem = pl.BlockSpec(memory_space=pltpu.SMEM)
    message = pl.pallas_call(
        pack_kernel,
        out_shape=jax.ShapeDtypeStruct((tables, queries, LANES), jnp.float32),
        in_specs=[smem, smem, vmem, vmem, vmem],
        out_specs=vmem,
        scratch_shapes=[pltpu.VMEM((queries * members, LANES), jnp.float32)],
        name="pack",
    )(table_slot, table_rows, raw_ids, id_weights, lengths)
    replicas = lax.axis_size("rep")
    split = message.reshape(tables * replicas, queries // replicas, LANES)
    received = exchange(split).reshape(message.shape)
    block = min(BLOCK_BAGS, tables * SUB // 2)
    pooled = pl.pallas_call(
        functools.partial(pool_kernel, width),
        out_shape=jax.ShapeDtypeStruct((tables * replicas, SUB, LANES), jnp.float32),
        in_specs=[smem, vmem, vmem],
        out_specs=vmem,
        scratch_shapes=[
            pltpu.VMEM((rows // LOW * SUB, SUB * HALF), jnp.bfloat16),
            pltpu.VMEM((LOW, SUB * HALF), jnp.bfloat16),
            pltpu.VMEM((2 * block, rows), jnp.bfloat16),
        ],
        name="pool",
    )(table_slot, received, embeddings)
    by_slot = exchange(pooled)
    return pl.pallas_call(
        place_kernel,
        out_shape=jax.ShapeDtypeStruct((queries, members, dim), jnp.float32),
        in_specs=[smem, vmem],
        out_specs=vmem,
        name="place",
    )(table_slot, by_slot)


def solution(mesh):
    in_specs = (
        P("tbl", None),
        P("tbl", "rep", None),
        P("tbl", "rep", None),
        P("tbl", "rep"),
        P(),
        P(),
    )
    out_specs = P("tbl", "rep", None)
    return jax.shard_map(
        per_device, mesh=mesh, in_specs=in_specs, out_specs=out_specs, check_vma=False
    )
```

time: 85.1 us -> 37.1 us (0.44)
  local copies, waits for them, and re-layouts: 37.3 us -> 0 us
  blocking collectives: 0 us -> 26.9 us
  waiting for transfers between devices: 21.4 us -> 0 us
  starting transfers between devices: 18.4 us -> 0 us
  Pallas kernels: 0 us -> 9.87 us
  other arithmetic: 3.98 us -> 0 us
  matrix products: 3.05 us -> 0 us
    gather x8 -> x0, local copies, waits for them, and re-layouts: 32.1 us -> none  [the longest x2 27.5 us: pool_block(): picked = jnp.take(embeddings, row_block, axis=0)]
    all_to_all x0 -> x2, blocking collectives: none -> 26.9 us  [exchange(): lax.all_to_all(array, ('tbl', 'rep'), split_axis=0, concat_axis=0, tiled=...]
    all_to_all x4 -> x0, waiting for transfers between devices: 21.4 us -> none  [the longest x1 7.77 us: per_device(): lax.all_to_all(pooled, 'tbl', split_axis=0, concat_axis=0, tiled=True)]
    all_to_all x4 -> x0, starting transfers between devices: 18.4 us -> none  [the longest x1 7.41 us: per_device(): lax.all_to_all(counts_sent, 'tbl', split_axis=0, concat_axis=0, tiled=True)]
    pallas_call x0 -> x3, Pallas kernels: none -> 9.87 us  [the longest x1 6.68 us: per_device(): pl.pallas_call(functools.partial(pool_kernel, width), out_shape=jax.Shape...]
    dot_general x1 -> x0, matrix products: 3.05 us -> none  [pool_block(): jnp.einsum('giqb,giqbd->giqd', scaled, picked.astype(jnp.float32), prefer...]
    unnamed x9 -> x0, local copies, waits for them, and re-layouts: 2.44 us -> none
    all_to_all x2 -> x0, other arithmetic: 1.39 us -> none  [the longest x1 0.69 us: per_device(): lax.all_to_all(weights_sent, 'tbl', split_axis=0, concat_axis=0, tiled=True)]
  transfers between devices with their start and end apart: 4 -> 0, of which waited for: 4 -> 0; matrix products, arithmetic and copies ran while one was open for 7% -> 0% of each run, Pallas kernels for 0% -> 0%
where the time goes in v1:
time: 37.1 us; the launch traced here: 36.8 us
  blocking collectives  26.9 us (73%)
  Pallas kernels  9.87 us (27%)
    all_to_all x2, blocking collectives, exchange(): lax.all_to_all(array, ('tbl', 'rep'), split_axis=0, concat_axis=0, tiled=...  26.9 us
    pallas_call x1, Pallas kernels, per_device(): pl.pallas_call(functools.partial(pool_kernel, width), out_shape=jax.Shape...  6.68 us
    pallas_call x1, Pallas kernels, per_device(): pl.pallas_call(place_kernel, out_shape=jax.ShapeDtypeStruct((queries, mem...  1.6 us
    pallas_call x1, Pallas kernels, per_device(): pl.pallas_call(pack_kernel, out_shape=jax.ShapeDtypeStruct((tables, queri...  1.59 us

profile of v1, /device:TPU:0, one launch (start us, length us, event | category | flops | bytes accessed | tf_op | source)
XLA Modules:
  0.0 36.8 jit_solution(14774204143172728509)
XLA Ops:
  0.0 1.6 %pack.1 = f32[16,8,128]{2,1,0:T(8,128)} custom-call(s32[16]{0:T(128)} %slot_ref.5, s32[16]{0:T(128)} %rows_ref.1, s32[8,8,60]{2,1,0:T(8,128)} %ids_ref.1, bf16[8,8,60]{2,1,0:T(8,128)(2,1)} %weights_ref.1, s32[8,8]{1,0:T(8,128)} %len_ref.1), custom_call_target="tpu_custom_call" | custom-call | tf_op jit(solution)/shard_map/pack/pallas_call | solution.py:144
  1.6 15.0 %all_to_all.10 = f32[32,4,128]{2,1,0:T(4,128)} all-to-all(f32[32,4,128]{2,1,0:T(4,128)} %bitcast.3), channel_id=1, replica_groups=mesh['rep'=2,'tbl'=16] {'tbl','rep'}, dimensions={0} | all-to-all | bytes 131072 | tf_op jit(solution)/shard_map/all_to_all | solution.py:135
  16.6 6.7 %pool.1 = f32[32,8,128]{2,1,0:T(8,128)} custom-call(s32[16]{0:T(128)} %slot_ref.5, f32[16,8,128]{2,1,0:T(8,128)} %bitcast.2, bf16[8192,256]{1,0:T(8,128)(2,1)} %emb_ref.1), custom_call_target="tpu_custom_call" | custom-call | tf_op jit(solution)/shard_map/pool/pallas_call | solution.py:156
  23.3 11.9 %all_to_all.11.by_slot_ref = f32[32,8,128]{2,1,0:T(8,128)} all-to-all(f32[32,8,128]{2,1,0:T(8,128)} %pool.1), channel_id=1, replica_groups=mesh['rep'=2,'tbl'=16] {'tbl','rep'}, dimensions={0} | all-to-all | bytes 262144 | tf_op jit(solution)/shard_map/all_to_all | solution.py:135
  35.2 1.6 %place.1 = f32[8,8,256]{2,1,0:T(8,128)} custom-call(s32[16]{0:T(128)} %slot_ref.5, f32[32,8,128]{2,1,0:T(8,128)} %all_to_all.11.by_slot_ref), custom_call_target="tpu_custom_call" | custom-call | tf_op jit(solution)/shard_map/place/pallas_call | solution.py:169

commit v2 on v1

--- a/solution.py
+++ b/solution.py
@@ -14,7 +14,23 @@
 BLOCK_BAGS = 64
 
 
-def pack_kernel(slot_ref, rows_ref, ids_ref, weights_ref, len_ref, out_ref, wide_ref):
+def fetch(pairs, sems):
+    copies = [pltpu.make_async_copy(src, dst, sems.at[i]) for i, (src, dst) in enumerate(pairs)]
+    for copy in copies:
+        copy.start()
+    for copy in copies:
+        copy.wait()
+
+
+def pack_kernel(
+    slot_hbm, rows_hbm, ids_hbm, weights_hbm, len_hbm, out_ref,
+    slot_ref, rows_ref, ids_ref, weights_ref, len_ref, wide_ref, sems,
+):
+    pairs = (
+        (slot_hbm, slot_ref), (rows_hbm, rows_ref), (ids_hbm, ids_ref),
+        (weights_hbm, weights_ref), (len_hbm, len_ref),
+    )
+    fetch(pairs, sems)
     queries, members, width = ids_ref.shape
     first = lax.axis_index("rep") * members
     wide_ref[:, 0:width] = weights_ref[...].reshape(queries * members, width).astype(jnp.float32)
@@ -35,7 +51,11 @@
         out_ref[slot, :, HALF : HALF + width] = weights
 
 
-def pool_kernel(width, slot_ref, msg_ref, emb_ref, out_ref, lhs_ref, rhs_ref, w_ref):
+def pool_kernel(width, slot_hbm, msg_ref, emb_hbm, out_ref, slot_ref, emb_ref, lhs_ref, rhs_ref, w_ref, sems):
+    slot_copy = pltpu.make_async_copy(slot_hbm, slot_ref, sems.at[0])
+    emb_copy = pltpu.make_async_copy(emb_hbm, emb_ref, sems.at[1])
+    slot_copy.start()
+    emb_copy.start()
     sources = msg_ref.shape[0]
     tables = slot_ref.shape[0]
     replicas = lax.axis_size("rep")
@@ -44,6 +64,7 @@
     def find(k, owner):
         return jnp.where(slot_ref[k] == here, k // (tables // replicas), owner)
 
+    slot_copy.wait()
     owner = lax.fori_loop(0, tables, find, jnp.int32(0))
     rows, dim = emb_ref.shape
     highs = rows // LOW
@@ -98,6 +119,7 @@
             return carry
 
         lax.fori_loop(0, groups, one_group, 0)
+        pl.when(index == 0)(emb_copy.wait)
         total = jnp.dot(w_ref[...], emb_ref[...], preferred_element_type=jnp.float32)
         for g in range(groups):
             msg = gather_group(base + 2 * g)
@@ -119,7 +141,8 @@
         lax.fori_loop(0, blocks, one_block, 0)
 
 
-def place_kernel(slot_ref, by_slot_ref, out_ref):
+def place_kernel(slot_hbm, by_slot_ref, out_ref, slot_ref, sems):
+    fetch(((slot_hbm, slot_ref),), sems)
     queries, members, dim = out_ref.shape
     first = lax.axis_index("rep") * members
     per = by_slot_ref.shape[1] // 2
@@ -136,17 +159,31 @@
 
 
 def per_device(embeddings, raw_ids, id_weights, lengths, table_slot, table_rows):
+    pinned = (embeddings, raw_ids, id_weights, lengths, table_slot, table_rows)
+    embeddings, raw_ids, id_weights, lengths, table_slot, table_rows = (
+        pltpu.with_memory_space_constraint(x, pltpu.HBM) for x in pinned
+    )
     queries, members, width = raw_ids.shape
     tables = table_slot.shape[0]
     rows, dim = embeddings.shape
     vmem = pl.BlockSpec(memory_space=pltpu.VMEM)
-    smem = pl.BlockSpec(memory_space=pltpu.SMEM)
+    hbm = pl.BlockSpec(memory_space=pltpu.HBM)
+    slots = pltpu.SMEM(table_slot.shape, jnp.int32)
     message = pl.pallas_call(
         pack_kernel,
         out_shape=jax.ShapeDtypeStruct((tables, queries, LANES), jnp.float32),
-        in_specs=[smem, smem, vmem, vmem, vmem],
+        in_specs=[hbm] * 5,
         out_specs=vmem,
-        scratch_shapes=[pltpu.VMEM((queries * members, LANES), jnp.float32)],
+        scratch_shapes=[
+            slots,
+            slots,
+            pltpu.VMEM(raw_ids.shape, raw_ids.dtype),
+            pltpu.VMEM(id_weights.shape, id_weights.dtype),
+            pltpu.VMEM(lengths.shape, lengths.dtype),
+            pltpu.VMEM((queries * members, LANES), jnp.float32),
+            pltpu.SemaphoreType.DMA((5,)),
+        ],
+        compiler_params=pltpu.CompilerParams(vmem_limit_bytes=2 << 20),
         name="pack",
     )(table_slot, table_rows, raw_ids, id_weights, lengths)
     replicas = lax.axis_size("rep")
@@ -156,21 +193,27 @@
     pooled = pl.pallas_call(
         functools.partial(pool_kernel, width),
         out_shape=jax.ShapeDtypeStruct((tables * replicas, SUB, LANES), jnp.float32),
-        in_specs=[smem, vmem, vmem],
+        in_specs=[hbm, vmem, hbm],
         out_specs=vmem,
         scratch_shapes=[
+            slots,
+            pltpu.VMEM(embeddings.shape, embeddings.dtype),
             pltpu.VMEM((rows // LOW * SUB, SUB * HALF), jnp.bfloat16),
             pltpu.VMEM((LOW, SUB * HALF), jnp.bfloat16),
             pltpu.VMEM((2 * block, rows), jnp.bfloat16),
+            pltpu.SemaphoreType.DMA((2,)),
         ],
+        compiler_params=pltpu.CompilerParams(vmem_limit_bytes=24 << 20),
         name="pool",
     )(table_slot, received, embeddings)
     by_slot = exchange(pooled)
     return pl.pallas_call(
         place_kernel,
         out_shape=jax.ShapeDtypeStruct((queries, members, dim), jnp.float32),
-        in_specs=[smem, vmem],
+        in_specs=[hbm, vmem],
         out_specs=vmem,
+        scratch_shapes=[slots, pltpu.SemaphoreType.DMA((1,))],
+        compiler_params=pltpu.CompilerParams(vmem_limit_bytes=2 << 20),
         name="place",
     )(table_slot, by_slot)
 

time: 37.1 us -> 32.1 us (0.87)
  Pallas kernels: 9.87 us -> 6.81 us
  blocking collectives: 26.9 us -> 25 us
    pallas_call x1, Pallas kernels: 6.68 us -> 4.5 us  [per_device(): pl.pallas_call(functools.partial(pool_kernel, width), out_shape=jax.Shape...]
    all_to_all x2, blocking collectives: 26.9 us -> 25 us  [exchange(): lax.all_to_all(array, ('tbl', 'rep'), split_axis=0, concat_axis=0, tiled=...]
    pallas_call x1, Pallas kernels: 1.59 us -> 0.96 us  [per_device(): pl.pallas_call(pack_kernel, out_shape=jax.ShapeDtypeStruct((tables, queri...]
where the time goes in v2:
time: 32.1 us; the launch traced here: 31.9 us
  blocking collectives  25 us (78%)
  Pallas kernels  6.81 us (21%)
    all_to_all x2, blocking collectives, exchange(): lax.all_to_all(array, ('tbl', 'rep'), split_axis=0, concat_axis=0, tiled=...  25 us
    pallas_call x1, Pallas kernels, per_device(): pl.pallas_call(functools.partial(pool_kernel, width), out_shape=jax.Shape...  4.5 us
    pallas_call x1, Pallas kernels, per_device(): pl.pallas_call(place_kernel, out_shape=jax.ShapeDtypeStruct((queries, mem...  1.35 us
    pallas_call x1, Pallas kernels, per_device(): pl.pallas_call(pack_kernel, out_shape=jax.ShapeDtypeStruct((tables, queri...  0.96 us

profile of v2, /device:TPU:0, one launch (start us, length us, event | category | flops | bytes accessed | tf_op | source)
XLA Modules:
  0.0 31.9 jit_solution(14850591041069537843)
XLA Ops:
  0.0 1.0 %pack.1 = f32[16,8,128]{2,1,0:T(8,128)S(1)} custom-call(s32[16]{0:T(128)} %slot_hbm.5, s32[16]{0:T(128)} %rows_hbm.1, s32[8,8,60]{2,1,0:T(8,128)} %ids_hbm.1, bf16[8,8,60]{2,1,0:T(8,128)(2,1)} %weights_hbm.1, s32[8,8]{1,0:T(8,128)} %len_hbm.1), custom_call_target="tpu_custom_call" | custom-call | tf_op jit(solution)/shard_map/pack/pallas_call | solution.py:172
  1.0 14.7 %all_to_all.10 = f32[32,4,128]{2,1,0:T(4,128)S(1)} all-to-all(f32[32,4,128]{2,1,0:T(4,128)S(1)} %bitcast.3), channel_id=1, replica_groups=mesh['rep'=2,'tbl'=16] {'tbl','rep'}, dimensions={0} | all-to-all | bytes 131072 | tf_op jit(solution)/shard_map/all_to_all | solution.py:158
  15.7 4.5 %pool.1 = f32[32,8,128]{2,1,0:T(8,128)S(1)} custom-call(s32[16]{0:T(128)} %slot_hbm.5, f32[16,8,128]{2,1,0:T(8,128)S(1)} %bitcast.2, bf16[8192,256]{1,0:T(8,128)(2,1)} %emb_hbm.1), custom_call_target="tpu_custom_call" | custom-call | tf_op jit(solution)/shard_map/pool/pallas_call | solution.py:193
  20.2 10.3 %all_to_all.11.by_slot_ref = f32[32,8,128]{2,1,0:T(8,128)S(1)} all-to-all(f32[32,8,128]{2,1,0:T(8,128)S(1)} %pool.1), channel_id=1, replica_groups=mesh['rep'=2,'tbl'=16] {'tbl','rep'}, dimensions={0} | all-to-all | bytes 262144 | tf_op jit(solution)/shard_map/all_to_all | solution.py:158
  30.5 1.4 %place.1 = f32[8,8,256]{2,1,0:T(8,128)} custom-call(s32[16]{0:T(128)} %slot_hbm.5, f32[32,8,128]{2,1,0:T(8,128)S(1)} %all_to_all.11.by_slot_ref), custom_call_target="tpu_custom_call" | custom-call | tf_op jit(solution)/shard_map/place/pallas_call | solution.py:210

commit v3 on v2

v3 whole, which is shorter than its diff:
```python
import functools

import jax
import jax.numpy as jnp
import numpy as np
from jax import lax
from jax.experimental import pallas as pl
from jax.experimental.pallas import tpu as pltpu
from jax.sharding import PartitionSpec as P

LANES = 128
HALF = 64
SUB = 8
LOW = 256
BLOCK_BAGS = 64
UNROLL = 4
CHUNKS = 8
ORDER_SEED = 217


def block_order(shards):
    return np.random.RandomState(ORDER_SEED).permutation(shards)


def fetch(pairs, sems):
    copies = [pltpu.make_async_copy(src, dst, sems.at[i]) for i, (src, dst) in enumerate(pairs)]
    for copy in copies:
        copy.start()
    for copy in copies:
        copy.wait()


def pack_kernel(
    place_hbm, slot_hbm, rows_hbm, ids_hbm, weights_hbm, len_hbm, out_ref, info_ref,
    place_ref, slot_ref, rows_ref, ids_ref, weights_ref, len_ref, wide_ref, sems,
):
    pairs = (
        (place_hbm, place_ref), (slot_hbm, slot_ref), (rows_hbm, rows_ref), (ids_hbm, ids_ref),
        (weights_hbm, weights_ref), (len_hbm, len_ref),
    )
    fetch(pairs, sems)
    queries, members, width = ids_ref.shape
    first = lax.axis_index("rep") * members
    wide_ref[:, 0:width] = weights_ref[...].reshape(queries * members, width).astype(jnp.float32)
    flat_ids = ids_ref.reshape(queries * members, width)
    position = lax.broadcasted_iota(jnp.int32, (queries, width), 1)
    counts = len_ref[...]
    out_ref[...] = jnp.zeros_like(out_ref)
    here = lax.axis_index("tbl")
    lane = lax.broadcasted_iota(jnp.int32, (1, LANES), 1)

    def find(k, owner):
        return jnp.where(slot_ref[k] == here, k // members, owner)

    owner = lax.fori_loop(0, slot_ref.shape[0], find, jnp.int32(0), unroll=slot_ref.shape[0] <= 16)
    info_ref[1:2, :] = jnp.full((1, LANES), owner, jnp.int32)
    mine = jnp.zeros((1, LANES), jnp.int32)
    for member in range(members):
        place = place_ref[slot_ref[first + member]]
        mine = jnp.where(lane == member, place, mine)
        rows = jnp.full((queries, width), rows_ref[first + member], jnp.int32).astype(jnp.float32)
        ids = flat_ids[pl.ds(member, queries, stride=members), :].astype(jnp.float32)
        local = ids - jnp.floor((ids + 0.5) * (1.0 / rows)) * rows
        count = counts[:, member : member + 1]
        weights = wide_ref[pl.ds(member, queries, stride=members), 0:width]
        weights = jnp.where(position < count, weights, 0.0)
        out_ref[place, :, 0:width] = local
        out_ref[place, :, width : width + 1] = count.astype(jnp.float32)
        out_ref[place, :, HALF : HALF + width] = weights
    info_ref[0:1, :] = mine


def pool_kernel(width, info_ref, msg_ref, emb_hbm, out_ref, emb_ref, w_ref, sems):
    rows, dim = emb_ref.shape
    highs = rows // LOW
    chunks = sems.shape[0]
    size = rows // chunks
    copies = [
        pltpu.make_async_copy(emb_hbm.at[pl.ds(c * size, size)], emb_ref.at[pl.ds(c * size, size)], sems.at[c])
        for c in range(chunks)
    ]
    for copy in copies:
        copy.start()
    sources = msg_ref.shape[0]
    replicas = lax.axis_size("rep")
    per = SUB // replicas
    block = min(BLOCK_BAGS, sources * per)
    groups = block // SUB
    lane = lax.broadcasted_iota(jnp.int32, (SUB, LANES), 1)
    sub = lax.broadcasted_iota(jnp.int32, (SUB, LANES), 0)
    left = lane < HALF
    upper = sub < per
    first_owner = jnp.broadcast_to(info_ref[1:2, :], (SUB, LANES)) == 0
    owns = [sub % per == jnp.where(left, 2 * m, 2 * m + 1) for m in range(2)]
    low_iota = lax.broadcasted_iota(jnp.int32, (LOW, LANES), 0).astype(jnp.float32).astype(jnp.bfloat16)

    def gather_group(start):
        one, two = msg_ref[start], msg_ref[start + 1]
        low_half = jnp.where(upper, one, pltpu.roll(two, per, 0))
        high_half = jnp.where(upper, pltpu.roll(one, per, 0), two)
        return jnp.where(first_owner, low_half, high_half)

    def spread_four(high, low, weights, flip, base):
        lhs, rhs = [], []
        shift = jnp.where(upper, 1.0, 0.0) if flip else jnp.where(upper, 0.0, 1.0)
        for m in range(2):
            h = jnp.where(owns[m], high - shift, -100.0)
            h = jnp.concatenate([h, h - 2.0], 0).astype(jnp.bfloat16)
            w = jnp.where(owns[m], weights, 0.0)
            w = jnp.concatenate([w, w], 0).astype(jnp.bfloat16)
            lhs.append(
                jnp.concatenate(
                    [jnp.where(h == jnp.bfloat16(top), w, jnp.bfloat16(0)) for top in range(0, highs, 4)], 0
                )
            )
            at = base + 2 * m
            row = jnp.where(left[0:1], low[at : at + 1], low[at + 1 : at + 2])
            row = jnp.broadcast_to(row, (2 * SUB, LANES)).astype(jnp.bfloat16)
            row = jnp.concatenate([row] * (LOW // (2 * SUB)), 0)
            rhs.append(jnp.where(low_iota == row, jnp.bfloat16(1), jnp.bfloat16(0)))
        return lax.dot_general(
            jnp.concatenate(lhs, 1), jnp.concatenate(rhs, 1), (((1,), (1,)), ((), ())),
            preferred_element_type=jnp.float32,
        )

    def one_block(index):
        base = index * (block // per)

        def one_group(g):
            msg = gather_group(base + 2 * g)
            turned = pltpu.roll(msg, HALF, 1)
            ids = jnp.where(left, msg, turned)
            weights = jnp.where(left, turned, msg)
            high = jnp.floor(ids * (1.0 / LOW))
            low = ids - high * LOW
            high_turned = pltpu.roll(high, per, 0)
            weights_turned = pltpu.roll(weights, per, 0)
            one = spread_four(
                jnp.where(upper, high, high_turned), low, jnp.where(upper, weights, weights_turned), False, 0
            )
            two = spread_four(
                jnp.where(upper, high_turned, high), low, jnp.where(upper, weights_turned, weights), True, per
            )
            at = pl.ds(pl.multiple_of(g * 2 * SUB, 2 * SUB), 2 * SUB)
            for v in range(highs // 2):
                for part in range(LOW // LANES):
                    cut = (slice(v * SUB, (v + 1) * SUB), slice(part * LANES, (part + 1) * LANES))
                    even = jnp.where(upper, one[cut], two[cut])
                    odd = jnp.where(upper, two[cut], one[cut])
                    both = jnp.concatenate([even, odd], 0)
                    rest = both - both.astype(jnp.bfloat16).astype(jnp.float32)
                    w_ref[0, v, part, at, :] = jnp.concatenate([even, rest[:SUB]], 0).astype(jnp.bfloat16)
                    w_ref[1, v, part, at, :] = jnp.concatenate([odd, rest[SUB:]], 0).astype(jnp.bfloat16)

        def body(g, carry):
            for u in range(UNROLL):
                one_group(g * UNROLL + u)
            return carry

        if groups == UNROLL:
            body(0, 0)
        else:
            lax.fori_loop(0, groups // UNROLL, body, 0)
        totals = [None, None]
        for c in range(chunks):
            pl.when(index == 0)(copies[c].wait)
            for parity in range(2):
                left_side, right_side = [], []
                for v in range(c * size // LOW // 2, (c + 1) * size // LOW // 2):
                    for part in range(LOW // LANES):
                        left_side.append(w_ref[parity, v, part])
                    at = (2 * v + parity) * LOW
                    right_side.append(emb_ref[at : at + LOW, :])
                term = jnp.dot(
                    jnp.concatenate(left_side, 1), jnp.concatenate(right_side, 0),
                    preferred_element_type=jnp.float32,
                )
                totals[parity] = term if c == 0 else totals[parity] + term
        for g in range(groups):
            msg = gather_group(base + 2 * g)
            at = 2 * SUB * g
            even, odd = (t[at : at + SUB] + t[at + SUB : at + 2 * SUB] for t in totals)
            pooled = (even + pltpu.roll(odd, per, 0)) / msg[:, width : width + 1]
            first, last = pooled[:, :LANES], pooled[:, LANES:]
            one = jnp.where(upper, first, pltpu.roll(last, per, 0))
            two = jnp.where(upper, pltpu.roll(first, per, 0), last)
            for replica in range(replicas):
                out_ref[(base + 2 * g) * replicas + replica] = one
                out_ref[(base + 2 * g + 1) * replicas + replica] = two

    blocks = sources * per // block
    if blocks == 1:
        one_block(0)
    else:
        pl.loop(0, blocks)(one_block)


def place_kernel(info_ref, by_slot_ref, out_ref):
    queries, members, dim = out_ref.shape
    per = by_slot_ref.shape[1] // 2
    upper = lax.broadcasted_iota(jnp.int32, by_slot_ref.shape[1:], 0) < per
    info = info_ref[0:1, :]
    for member in range(members):
        place = info[0, member]
        one, two = by_slot_ref[2 * place], by_slot_ref[2 * place + 1]
        out_ref[:, member, :LANES] = jnp.where(upper, one, pltpu.roll(two, per, 0))
        out_ref[:, member, LANES:] = jnp.where(upper, pltpu.roll(one, per, 0), two)


def exchange(array):
    shards, replicas = lax.axis_size("tbl"), lax.axis_size("rep")
    group = [int(shard) + shards * replica for shard in block_order(shards) for replica in range(replicas)]
    return lax.all_to_all(
        array, ("rep", "tbl"), split_axis=0, concat_axis=0, axis_index_groups=[group], tiled=True
    )


def per_device(embeddings, raw_ids, id_weights, lengths, table_slot, table_rows):
    places = jnp.asarray(np.argsort(block_order(lax.axis_size("tbl"))), jnp.int32)
    pinned = (embeddings, raw_ids, id_weights, lengths, table_slot, table_rows, places)
    embeddings, raw_ids, id_weights, lengths, table_slot, table_rows, places = (
        pltpu.with_memory_space_constraint(x, pltpu.HBM) for x in pinned
    )
    queries, members, width = raw_ids.shape
    tables = table_slot.shape[0]
    rows, dim = embeddings.shape
    vmem = pl.BlockSpec(memory_space=pltpu.VMEM)
    hbm = pl.BlockSpec(memory_space=pltpu.HBM)
    slots = pltpu.SMEM(table_slot.shape, jnp.int32)
    message, info = pl.pallas_call(
        pack_kernel,
        out_shape=(
            jax.ShapeDtypeStruct((tables, queries, LANES), jnp.float32),
            jax.ShapeDtypeStruct((SUB, LANES), jnp.int32),
        ),
        in_specs=[hbm] * 6,
        out_specs=(vmem, vmem),
        scratch_shapes=[
            slots,
            slots,
            slots,
            pltpu.VMEM(raw_ids.shape, raw_ids.dtype),
            pltpu.VMEM(id_weights.shape, id_weights.dtype),
            pltpu.VMEM(lengths.shape, lengths.dtype),
            pltpu.VMEM((queries * members, LANES), jnp.float32),
            pltpu.SemaphoreType.DMA((6,)),
        ],
        compiler_params=pltpu.CompilerParams(vmem_limit_bytes=4 << 20),
        name="pack",
    )(places, table_slot, table_rows, raw_ids, id_weights, lengths)
    replicas = lax.axis_size("rep")
    split = message.reshape(tables * replicas, queries // replicas, LANES)
    received = exchange(split).reshape(message.shape)
    block = min(BLOCK_BAGS, tables * SUB // 2)
    pooled = pl.pallas_call(
        functools.partial(pool_kernel, width),
        out_shape=jax.ShapeDtypeStruct((tables * replicas, SUB, LANES), jnp.float32),
        in_specs=[vmem, vmem, hbm],
        out_specs=vmem,
        scratch_shapes=[
            pltpu.VMEM(embeddings.shape, embeddings.dtype),
            pltpu.VMEM((2, rows // LOW // 2, LOW // LANES, 2 * block, LANES), jnp.bfloat16),
            pltpu.SemaphoreType.DMA((CHUNKS,)),
        ],
        compiler_params=pltpu.CompilerParams(vmem_limit_bytes=24 << 20),
        name="pool",
    )(info, received, embeddings)
    by_slot = exchange(pooled)
    return pl.pallas_call(
        place_kernel,
        out_shape=jax.ShapeDtypeStruct((queries, members, dim), jnp.float32),
        in_specs=[vmem, vmem],
        out_specs=vmem,
        compiler_params=pltpu.CompilerParams(vmem_limit_bytes=4 << 20),
        name="place",
    )(info, by_slot)


def solution(mesh):
    in_specs = (
        P("tbl", None),
        P("tbl", "rep", None),
        P("tbl", "rep", None),
        P("tbl", "rep"),
        P(),
        P(),
    )
    out_specs = P("tbl", "rep", None)
    return jax.shard_map(
        per_device, mesh=mesh, in_specs=in_specs, out_specs=out_specs, check_vma=False
    )
```

time: 32.1 us -> 27.7 us (0.86)
  Pallas kernels: 6.81 us -> 4.2 us
  blocking collectives: 25 us -> 23.2 us
    pallas_call x1, Pallas kernels: 4.5 us -> 2.46 us  [per_device(): pl.pallas_call(functools.partial(pool_kernel, width), out_shape=jax.Shape...]
    all_to_all x2, blocking collectives: 25 us -> 23.2 us  [exchange(): lax.all_to_all(array, ('rep', 'tbl'), split_axis=0, concat_axis=0, axis_i...]
    pallas_call x1, Pallas kernels: 1.35 us -> 0.77 us  [per_device(): pl.pallas_call(place_kernel, out_shape=jax.ShapeDtypeStruct((queries, mem...]
where the time goes in v3:
time: 27.7 us; the launch traced here: 27.4 us
  blocking collectives  23.2 us (84%)
  Pallas kernels  4.2 us (15%)
    all_to_all x2, blocking collectives, exchange(): lax.all_to_all(array, ('rep', 'tbl'), split_axis=0, concat_axis=0, axis_i...  23.2 us
    pallas_call x1, Pallas kernels, per_device(): pl.pallas_call(functools.partial(pool_kernel, width), out_shape=jax.Shape...  2.46 us
    pallas_call x1, Pallas kernels, per_device(): pl.pallas_call(pack_kernel, out_shape=(jax.ShapeDtypeStruct((tables, quer...  0.97 us
    pallas_call x1, Pallas kernels, per_device(): pl.pallas_call(place_kernel, out_shape=jax.ShapeDtypeStruct((queries, mem...  0.77 us

profile of v3, /device:TPU:0, one launch (start us, length us, event | category | flops | bytes accessed | tf_op | source)
XLA Modules:
  0.0 27.4 jit_solution(13104342670049461222)
XLA Ops:
  0.0 1.0 %pack.1 = (f32[16,8,128]{2,1,0:T(8,128)S(1)}, s32[8,128]{1,0:T(8,128)S(1)}) custom-call(s32[16]{0:T(128)} %constant.2.clone.place_hbm, s32[16]{0:T(128)} %slot_hbm.1, s32[16]{0:T(128)} %rows_hbm.1, s32[8,8,60]{2,1,0:T(8,128)} %ids_hbm.1, bf16[8,8,60]{2,1,0:T(8,128)(2,1)} %weights_hbm.1, s32[8,8]{1,0:T(8,128)} %len_hbm.1), custom_call_target="tpu_custom_call" | custom-call | tf_op jit(solution)/shard_map/pack/pallas_call | solution.py:230
  1.0 14.3 %all_to_all.10 = f32[32,4,128]{2,1,0:T(4,128)S(1)} all-to-all(f32[32,4,128]{2,1,0:T(4,128)S(1)} %bitcast.3), channel_id=1, replica_groups={{7,23,13,29,14,30,4,20,15,31,10,26,3,19,1,17,0,16,11,27,8,24,5,21,6,22,..., dimensions={0} | all-to-all | bytes 131072 | tf_op jit(solution)/shard_map/all_to_all | solution.py:213
  15.2 2.5 %pool.1 = f32[32,8,128]{2,1,0:T(8,128)S(1)} custom-call(s32[8,128]{1,0:T(8,128)S(1)} %get-tuple-element.7.info_ref, f32[16,8,128]{2,1,0:T(8,128)S(1)} %bitcast.2, bf16[8192,256]{1,0:T(8,128)(2,1)} %emb_hbm.1), custom_call_target="tpu_custom_call" | custom-call | tf_op jit(solution)/shard_map/pool/pallas_call | solution.py:255
  17.7 9.0 %all_to_all.11.by_slot_ref = f32[32,8,128]{2,1,0:T(8,128)S(1)} all-to-all(f32[32,8,128]{2,1,0:T(8,128)S(1)} %pool.1), channel_id=1, replica_groups={{7,23,13,29,14,30,4,20,15,31,10,26,3,19,1,17,0,16,11,27,8,24,5,21,6,22,..., dimensions={0} | all-to-all | bytes 262144 | tf_op jit(solution)/shard_map/all_to_all | solution.py:213
  26.7 0.8 %place.1 = f32[8,8,256]{2,1,0:T(8,128)} custom-call(s32[8,128]{1,0:T(8,128)S(1)} %get-tuple-element.7.info_ref, f32[32,8,128]{2,1,0:T(8,128)S(1)} %all_to_all.11.by_slot_ref), custom_call_target="tpu_custom_call" | custom-call | tf_op jit(solution)/shard_map/place/pallas_call | solution.py:269

commit v4 on v3

--- a/solution.py
+++ b/solution.py
@@ -15,6 +15,7 @@
 BLOCK_BAGS = 64
 UNROLL = 4
 CHUNKS = 8
+PREFIXES = (4, 6, 8)
 ORDER_SEED = 217
 
 
@@ -49,11 +50,12 @@
     here = lax.axis_index("tbl")
     lane = lax.broadcasted_iota(jnp.int32, (1, LANES), 1)
 
-    def find(k, owner):
-        return jnp.where(slot_ref[k] == here, k // members, owner)
-
-    owner = lax.fori_loop(0, slot_ref.shape[0], find, jnp.int32(0), unroll=slot_ref.shape[0] <= 16)
-    info_ref[1:2, :] = jnp.full((1, LANES), owner, jnp.int32)
+    def find(k, table):
+        return jnp.where(slot_ref[k] == here, k, table)
+
+    table = lax.fori_loop(0, slot_ref.shape[0], find, jnp.int32(0), unroll=slot_ref.shape[0] <= 16)
+    info_ref[1:2, :] = jnp.full((1, LANES), table // members, jnp.int32)
+    info_ref[2:3, :] = jnp.full((1, LANES), rows_ref[table], jnp.int32)
     mine = jnp.zeros((1, LANES), jnp.int32)
     for member in range(members):
         place = place_ref[slot_ref[first + member]]
@@ -79,8 +81,22 @@
         pltpu.make_async_copy(emb_hbm.at[pl.ds(c * size, size)], emb_ref.at[pl.ds(c * size, size)], sems.at[c])
         for c in range(chunks)
     ]
-    for copy in copies:
+    for copy in copies[: PREFIXES[0]]:
         copy.start()
+    used = info_ref[2:3, :][0, 0]
+
+    def within(part):
+        low_end = 0 if part == 0 else PREFIXES[part - 1] * size
+        above = used > low_end
+        return above if part == len(PREFIXES) - 1 else above & (used <= PREFIXES[part] * size)
+
+    for part in range(1, len(PREFIXES)):
+
+        @pl.when(used > PREFIXES[part - 1] * size)
+        def _(part=part):
+            for copy in copies[PREFIXES[part - 1] : PREFIXES[part]]:
+                copy.start()
+
     sources = msg_ref.shape[0]
     replicas = lax.axis_size("rep")
     per = SUB // replicas
@@ -161,8 +177,12 @@
             body(0, 0)
         else:
             lax.fori_loop(0, groups // UNROLL, body, 0)
+        for part, count in enumerate(PREFIXES):
+            pl.when(within(part))(functools.partial(finish, index, base, count))
+
+    def finish(index, base, count):
         totals = [None, None]
-        for c in range(chunks):
+        for c in range(count):
             pl.when(index == 0)(copies[c].wait)
             for parity in range(2):
                 left_side, right_side = [], []

time: 27.7 us -> 27.4 us (0.989); the launches traced: 27.4 us -> 27.5 us
  no operation moved by 1% of the time
where the time goes in v4:
time: 27.4 us; the launch traced here: 27.5 us
  blocking collectives  23.2 us (85%)
  Pallas kernels  4.2 us (15%)
    all_to_all x2, blocking collectives, exchange(): lax.all_to_all(array, ('rep', 'tbl'), split_axis=0, concat_axis=0, axis_i...  23.2 us
    pallas_call x1, Pallas kernels, per_device(): pl.pallas_call(functools.partial(pool_kernel, width), out_shape=jax.Shape...  2.47 us
    pallas_call x1, Pallas kernels, per_device(): pl.pallas_call(pack_kernel, out_shape=(jax.ShapeDtypeStruct((tables, quer...  0.97 us
    pallas_call x1, Pallas kernels, per_device(): pl.pallas_call(place_kernel, out_shape=jax.ShapeDtypeStruct((queries, mem...  0.77 us

profile of v4, /device:TPU:0, one launch (start us, length us, event | category | flops | bytes accessed | tf_op | source)
XLA Modules:
  0.0 27.5 jit_solution(13159651757517174019)
XLA Ops:
  0.0 1.0 %pack.1 = (f32[16,8,128]{2,1,0:T(8,128)S(1)}, s32[8,128]{1,0:T(8,128)S(1)}) custom-call(s32[16]{0:T(128)} %constant.2.clone.place_hbm, s32[16]{0:T(128)} %slot_hbm.1, s32[16]{0:T(128)} %rows_hbm.1, s32[8,8,60]{2,1,0:T(8,128)} %ids_hbm.1, bf16[8,8,60]{2,1,0:T(8,128)(2,1)} %weights_hbm.1, s32[8,8]{1,0:T(8,128)} %len_hbm.1), custom_call_target="tpu_custom_call" | custom-call | tf_op jit(solution)/shard_map/pack/pallas_call | solution.py:250
  1.0 14.3 %all_to_all.10 = f32[32,4,128]{2,1,0:T(4,128)S(1)} all-to-all(f32[32,4,128]{2,1,0:T(4,128)S(1)} %bitcast.3), channel_id=1, replica_groups={{7,23,13,29,14,30,4,20,15,31,10,26,3,19,1,17,0,16,11,27,8,24,5,21,6,22,..., dimensions={0} | all-to-all | bytes 131072 | tf_op jit(solution)/shard_map/all_to_all | solution.py:233
  15.2 2.5 %pool.1 = f32[32,8,128]{2,1,0:T(8,128)S(1)} custom-call(s32[8,128]{1,0:T(8,128)S(1)} %get-tuple-element.7.info_ref, f32[16,8,128]{2,1,0:T(8,128)S(1)} %bitcast.2, bf16[8192,256]{1,0:T(8,128)(2,1)} %emb_hbm.1), custom_call_target="tpu_custom_call" | custom-call | tf_op jit(solution)/shard_map/pool/pallas_call | solution.py:275
  17.7 9.0 %all_to_all.11.by_slot_ref = f32[32,8,128]{2,1,0:T(8,128)S(1)} all-to-all(f32[32,8,128]{2,1,0:T(8,128)S(1)} %pool.1), channel_id=1, replica_groups={{7,23,13,29,14,30,4,20,15,31,10,26,3,19,1,17,0,16,11,27,8,24,5,21,6,22,..., dimensions={0} | all-to-all | bytes 262144 | tf_op jit(solution)/shard_map/all_to_all | solution.py:233
  26.7 0.8 %place.1 = f32[8,8,256]{2,1,0:T(8,128)} custom-call(s32[8,128]{1,0:T(8,128)S(1)} %get-tuple-element.7.info_ref, f32[32,8,128]{2,1,0:T(8,128)S(1)} %all_to_all.11.by_slot_ref), custom_call_target="tpu_custom_call" | custom-call | tf_op jit(solution)/shard_map/place/pallas_call | solution.py:289

commit v5 on v4

--- a/solution.py
+++ b/solution.py
@@ -16,7 +16,7 @@
 UNROLL = 4
 CHUNKS = 8
 PREFIXES = (4, 6, 8)
-ORDER_SEED = 217
+ORDER_SEED = 1018
 
 
 def block_order(shards):

time: 27.4 us -> 27.1 us (0.989)
  Pallas kernels: 4.2 us -> 3.63 us
    pallas_call x1, Pallas kernels: 2.47 us -> 1.89 us  [per_device(): pl.pallas_call(functools.partial(pool_kernel, width), out_shape=jax.Shape...]
where the time goes in v5:
time: 27.1 us; the launch traced here: 26.9 us
  blocking collectives  23.3 us (86%)
  Pallas kernels  3.63 us (13%)
    all_to_all x2, blocking collectives, exchange(): lax.all_to_all(array, ('rep', 'tbl'), split_axis=0, concat_axis=0, axis_i...  23.3 us
    pallas_call x1, Pallas kernels, per_device(): pl.pallas_call(functools.partial(pool_kernel, width), out_shape=jax.Shape...  1.89 us
    pallas_call x1, Pallas kernels, per_device(): pl.pallas_call(pack_kernel, out_shape=(jax.ShapeDtypeStruct((tables, quer...  0.97 us
    pallas_call x1, Pallas kernels, per_device(): pl.pallas_call(place_kernel, out_shape=jax.ShapeDtypeStruct((queries, mem...  0.77 us

profile of v5, /device:TPU:0, one launch (start us, length us, event | category | flops | bytes accessed | tf_op | source)
XLA Modules:
  0.0 26.9 jit_solution(8815157836611521904)
XLA Ops:
  0.0 1.0 %pack.1 = (f32[16,8,128]{2,1,0:T(8,128)S(1)}, s32[8,128]{1,0:T(8,128)S(1)}) custom-call(s32[16]{0:T(128)} %constant.2.clone.place_hbm, s32[16]{0:T(128)} %slot_hbm.1, s32[16]{0:T(128)} %rows_hbm.1, s32[8,8,60]{2,1,0:T(8,128)} %ids_hbm.1, bf16[8,8,60]{2,1,0:T(8,128)(2,1)} %weights_hbm.1, s32[8,8]{1,0:T(8,128)} %len_hbm.1), custom_call_target="tpu_custom_call" | custom-call | tf_op jit(solution)/shard_map/pack/pallas_call | solution.py:250
  1.0 14.3 %all_to_all.10 = f32[32,4,128]{2,1,0:T(4,128)S(1)} all-to-all(f32[32,4,128]{2,1,0:T(4,128)S(1)} %bitcast.3), channel_id=1, replica_groups={{12,28,1,17,8,24,6,22,3,19,2,18,0,16,14,30,13,29,4,20,10,26,7,23,5,21,1..., dimensions={0} | all-to-all | bytes 131072 | tf_op jit(solution)/shard_map/all_to_all | solution.py:233
  15.2 1.9 %pool.1 = f32[32,8,128]{2,1,0:T(8,128)S(1)} custom-call(s32[8,128]{1,0:T(8,128)S(1)} %get-tuple-element.7.info_ref, f32[16,8,128]{2,1,0:T(8,128)S(1)} %bitcast.2, bf16[8192,256]{1,0:T(8,128)(2,1)} %emb_hbm.1), custom_call_target="tpu_custom_call" | custom-call | tf_op jit(solution)/shard_map/pool/pallas_call | solution.py:275
  17.1 9.0 %all_to_all.11.by_slot_ref = f32[32,8,128]{2,1,0:T(8,128)S(1)} all-to-all(f32[32,8,128]{2,1,0:T(8,128)S(1)} %pool.1), channel_id=1, replica_groups={{12,28,1,17,8,24,6,22,3,19,2,18,0,16,14,30,13,29,4,20,10,26,7,23,5,21,1..., dimensions={0} | all-to-all | bytes 262144 | tf_op jit(solution)/shard_map/all_to_all | solution.py:233
  26.1 0.8 %place.1 = f32[8,8,256]{2,1,0:T(8,128)} custom-call(s32[8,128]{1,0:T(8,128)S(1)} %get-tuple-element.7.info_ref, f32[32,8,128]{2,1,0:T(8,128)S(1)} %all_to_all.11.by_slot_ref), custom_call_target="tpu_custom_call" | custom-call | tf_op jit(solution)/shard_map/place/pallas_call | solution.py:289
